TPU v7x, 32 devices: a whole 2x2x4 slice. The times are simulated.
32 devices in a mesh: dp: 8 (over z, core), tensor: 4 (over y, x).
Axes of the slice: x: 2, y: 2, z: 4, core: 2. Of those that a mesh axis runs over, the one named last changes fastest.
Arguments:
- tokens_in: bfloat16 [1024, 8192], P(('dp', 'tensor')), may hold values from -6 to 6
- projector: bfloat16 [8192, 512], P('tensor'), may hold values from -0.0625 to 0.0625
- gate_pre: bfloat16 [1024, 15360], P('dp', 'tensor'), may hold values from -6 to 6
- up_pre: bfloat16 [1024, 15360], P('dp', 'tensor'), may hold values from -6 to 6
- hidden_grad: bfloat16 [1024, 15360], P('dp', 'tensor'), may hold values from -6 to 6
- moment_m: float32 [15360, 1024], P(('tensor', 'dp')), may hold values from -4 to 4
- moment_v: float32 [15360, 1024], P(('tensor', 'dp')), may hold values from 0.05 to 1
Outputs:
- m_next: float32 [15360, 1024], P(('tensor', 'dp'))
- v_next: float32 [15360, 1024], P(('tensor', 'dp'))
- direction: float32 [15360, 1024], P(('tensor', 'dp'))
All inputs are finite; a program needn't handle non-finite values.
Results may differ from a plain program's by a relative error of at most 0.00098.
Values may be sent and summed in bfloat16 or wider, within the bound.
A program may use at most 64 MiB of HBM per device.

v0:
```python
import jax
import jax.numpy as jnp
from jax import lax
from jax.sharding import PartitionSpec as P


def local(tokens_in, projector, gate_pre, up_pre, hidden_grad, moment_m, moment_v):
    columns = lax.all_to_all(tokens_in, "tensor", split_axis=1, concat_axis=0, tiled=True)
    partial_xp = jnp.dot(columns, projector, preferred_element_type=jnp.float32)
    own_rows = lax.psum_scatter(partial_xp, "tensor", scatter_dimension=0, tiled=True).astype(
        jnp.bfloat16
    )
    xp = lax.all_gather(own_rows, "tensor", axis=0, tiled=True)
    gate = gate_pre.astype(jnp.float32)
    hgrad = hidden_grad.astype(jnp.float32)
    sig = jax.nn.sigmoid(gate)
    contract = (((0,), (0,)), ((), ()))
    upval = up_pre.astype(jnp.float32)
    grad_gate = (hgrad * upval * sig * (1.0 + gate * (1.0 - sig))).astype(jnp.bfloat16)
    gate_half = lax.psum_scatter(
        lax.dot_general(grad_gate, xp, contract, preferred_element_type=jnp.float32),
        "dp",
        scatter_dimension=0,
        tiled=True,
    )
    grad_up = (hgrad * gate * sig).astype(jnp.bfloat16)
    up_half = lax.psum_scatter(
        lax.dot_general(grad_up, xp, contract, preferred_element_type=jnp.float32),
        "dp",
        scatter_dimension=0,
        tiled=True,
    )
    summed = jnp.concatenate([gate_half, up_half], axis=1)
    groups = lax.axis_size("dp")
    total_tokens = gate_pre.shape[0] * groups
    proj = summed * float(total_tokens) ** (-0.5)
    m_next = 0.9 * moment_m + 0.1 * proj
    v_next = 0.95 * moment_v + 0.05 * proj * proj
    direction = m_next / (jnp.sqrt(v_next) + 1e-08)
    return (m_next, v_next, direction)


def solution(mesh):
    return jax.shard_map(
        local,
        mesh=mesh,
        in_specs=(
            P(("dp", "tensor"), None),
            P("tensor", None),
            P("dp", "tensor"),
            P("dp", "tensor"),
            P("dp", "tensor"),
            P(("tensor", "dp"), None),
            P(("tensor", "dp"), None),
        ),
        out_specs=(P(("tensor", "dp"), None), P(("tensor", "dp"), None), P(("tensor", "dp"), None)),
        check_vma=False,
    )
```

profile of v0, /device:TPU:0, one launch (start us, length us, event | category | flops | bytes accessed | tf_op | source)
XLA Modules:
  0.0 247.1 jit_solution(16418651539253700325)
XLA Ops:
  7.2 0.0 copy-start
  7.2 0.0 reduce-scatter.4.cloned.1.call-start
  7.2 1.2 copy.14
  8.4 13.5 %all_to_all.19 = bf16[32,4,2048]{2,0,1:T(8,128)(2,1)S(1)} all-to-all(bf16[32,4,2048]{2,0,1:T(8,128)(2,1)S(1)} %bitcast.11), channel_id=1, replica_groups=mesh['dp'=8,'tensor'=4] {'tensor'}, dimensions={1} | all-to-all | bytes 1048576 | tf_op jit(solution)/shard_map/all_to_all | solution.py:8
  22.0 0.0 copy-done
  22.0 1.2 fusion.17
  23.1 0.0 reduce-scatter.4.cloned.1.call-update
  23.1 0.0 reduce-scatter.6.cloned.1.call-start
  23.2 24.2 %reduce-scatter.4.cloned.1.call-done = f32[32,512]{1,0:T(8,128)} async-done(((f32[128,512]{1,0:T(8,128)}), f32[32,512]{1,0:T(8,128)}) %reduce-scatter.4.cloned.1.call-update) | async-done | bytes 65552 | tf_op jit(solution)/shard_map/reduce_scatter | solution.py:10
  47.4 0.8 convert_element_type.22
  48.2 8.5 %all_gather.3 = bf16[128,512]{1,0:T(8,128)(2,1)S(1)} all-gather(bf16[32,512]{1,0:T(8,128)(2,1)S(1)} %convert_element_type.22), channel_id=1, replica_groups=mesh['dp'=8,'tensor'=4] {'tensor'}, dimensions={0}, use_global_device_ids=true | all-gather | bytes 163840 | tf_op jit(solution)/shard_map/all_gather | solution.py:13
  56.7 0.0 copy-done.2
  56.7 5.8 %fusion.11 = f32[3840,512]{1,0:T(8,128)} fusion(bf16[128,512]{1,0:T(8,128)(2,1)S(1)} %all_gather.3, bf16[128,3840]{1,0:T(8,128)(2,1)} %param.11, bf16[128,3840]{1,0:T(8,128)(2,1)} %param.9, bf16[128,3840]{1,0:T(8,128)(2,1)S(1)} %copy-done.2), kind=kOutput, calls=%fused_computation.17 | convolution fusion | flops 509706240 | bytes 10944512 | tf_op jit(solution)/shard_map/dot_general | solution.py:21
  62.5 0.0 reduce-scatter.6.cloned.1.call-update
  62.5 0.0 reduce-scatter.8.cloned.1.call-start
  62.6 1.1 copy-done.3
  63.7 5.8 %fusion.9 = f32[3840,512]{1,0:T(8,128)} fusion(bf16[128,512]{1,0:T(8,128)(2,1)S(1)} %all_gather.3, bf16[128,3840]{1,0:T(8,128)(2,1)} %param.9, bf16[128,3840]{1,0:T(8,128)(2,1)S(1)} %copy-done.3), kind=kOutput, calls=%fused_computation.16 | convolution fusion | flops 507248640 | bytes 9961472 | tf_op jit(solution)/shard_map/dot_general | solution.py:28
  69.5 0.0 reduce-scatter.8.cloned.1.call-update
  69.5 77.8 %reduce-scatter.6.cloned.1.call-done = f32[480,512]{1,0:T(8,128)} async-done(((f32[3840,512]{1,0:T(8,128)}), f32[480,512]{1,0:T(8,128)}) %reduce-scatter.6.cloned.1.call-update) | async-done | bytes 983056 | tf_op jit(solution)/shard_map/reduce_scatter | solution.py:20
  147.3 2.2 constant_dynamic-update-slice_fusion.1
  149.5 83.2 %reduce-scatter.8.cloned.1.call-done = f32[480,512]{1,0:T(8,128)} async-done(((f32[3840,512]{1,0:T(8,128)}), f32[480,512]{1,0:T(8,128)}) %reduce-scatter.8.cloned.1.call-update) | async-done | bytes 983056 | tf_op jit(solution)/shard_map/reduce_scatter | solution.py:27
  232.6 2.4 constant_dynamic-update-slice_fusion
  235.0 0.0 copy-done.1
  235.0 5.5 %add_divide_fusion = (f32[480,1024]{1,0:T(8,128)}, f32[480,1024]{1,0:T(8,128)}, f32[480,1024]{1,0:T(8,128)}) fusion(f32[480,1024]{1,0:T(8,128)} %constant_dynamic-update-slice_fusion, f32[480,1024]{1,0:T(8,128)S(1)} %copy-done.1, f32[480,1024]{1,0:T(8,128)} %param.12), kind=kLoop, calls=%fused_computation.13 | loop fusion | flops 4915200 | bytes 11796480 | tf_op jit(solution)/shard_map/div | solution.py:39
  (3 shorter events, 0.0 us)
Async XLA Ops:
  7.2 14.8 %copy-start = (bf16[2048,512]{1,0:T(8,128)(2,1)S(1)}, bf16[2048,512]{1,0:T(8,128)(2,1)}, u32[]{:S(2)}) copy-start(bf16[2048,512]{1,0:T(8,128)(2,1)} %param.8) | copy-start | bytes 6291460
  7.2 40.2 %reduce-scatter.4.cloned.1.call-start = ((), (), s32[]{:S(2)}) async-start(), calls=%async_computation.4 | async-start | bytes 327680 | tf_op jit(solution)/shard_map/reduce_scatter | solution.py:10
  22.0 34.7 %copy-start.2 = (bf16[128,3840]{1,0:T(8,128)(2,1)S(1)}, bf16[128,3840]{1,0:T(8,128)(2,1)}, u32[]{:S(2)}) copy-start(bf16[128,3840]{1,0:T(8,128)(2,1)} %param.10) | copy-start | bytes 2949124
  23.1 124.1 %reduce-scatter.6.cloned.1.call-start = ((), (), s32[]{:S(2)}) async-start(), calls=%async_computation.5 | async-start | bytes 8847360 | tf_op jit(solution)/shard_map/reduce_scatter | solution.py:20
  62.5 1.2 copy-start.3
  62.5 170.1 %reduce-scatter.8.cloned.1.call-start = ((), (), s32[]{:S(2)}) async-start(), calls=%async_computation.6 | async-start | bytes 8847360 | tf_op jit(solution)/shard_map/reduce_scatter | solution.py:27
  232.6 2.4 copy-start.1
Sparse Core Ops, SparseCore 0:
  23.3 24.0 reduce-scatter.3
  62.7 84.5 reduce-scatter.5
  149.6 83.0 reduce-scatter.7
where the time goes:
time: 247 us
  waiting for transfers between devices  185 us (75%)
  blocking collectives  22 us (9%)
  between operations  13.8 us (6%)
  matrix products  12.8 us (5%)
  local copies, waits for them, and re-layouts  6.92 us (3%)
  other arithmetic  6.38 us (3%)
    reduce_scatter x1, waiting for transfers between devices, local(): lax.psum_scatter(lax.dot_general(grad_up, xp, contract, preferred_element...  83.2 us
    reduce_scatter x1, waiting for transfers between devices, local(): lax.psum_scatter(lax.dot_general(grad_gate, xp, contract, preferred_eleme...  77.8 us
    reduce_scatter x1, waiting for transfers between devices, local(): lax.psum_scatter(partial_xp, 'tensor', scatter_dimension=0, tiled=True)  24.2 us
    all_to_all x1, blocking collectives, local(): lax.all_to_all(tokens_in, 'tensor', split_axis=1, concat_axis=0, tiled=True)  13.5 us
    all_gather x1, blocking collectives, local(): xp = lax.all_gather(own_rows, 'tensor', axis=0, tiled=True)  8.46 us
    dot_general x1, matrix products, local(): lax.dot_general(grad_gate, xp, contract, preferred_element_type=jnp.float32)  5.82 us
    dot_general x1, matrix products, local(): lax.dot_general(grad_up, xp, contract, preferred_element_type=jnp.float32)  5.78 us
    div x1, other arithmetic, local(): direction = m_next / (jnp.sqrt(v_next) + 1e-08)  5.54 us
  transfers between devices with their start and end apart: 3, of which 3 were waited for; matrix products, arithmetic and copies ran while one was open for 3% of the time, Pallas kernels for 0%

commit v1 on v0

v1 whole, which is shorter than its diff:
```python
import jax
import jax.numpy as jnp
from jax import lax
from jax.sharding import PartitionSpec as P


def finish(summed, total_tokens, moment_m, moment_v):
    proj = summed * float(total_tokens) ** (-0.5)
    m_next = 0.9 * moment_m + 0.1 * proj
    v_next = 0.95 * moment_v + 0.05 * proj * proj
    direction = m_next / (jnp.sqrt(v_next) + 1e-08)
    return (m_next, v_next, direction)


def local(tokens_in, projector, gate_pre, up_pre, hidden_grad, moment_m, moment_v):
    gate = gate_pre.astype(jnp.float32)
    hgrad = hidden_grad.astype(jnp.float32)
    sig = jax.nn.sigmoid(gate)
    upval = up_pre.astype(jnp.float32)
    grad_gate = (hgrad * upval * sig * (1.0 + gate * (1.0 - sig))).astype(jnp.bfloat16)
    grad_up = (hgrad * gate * sig).astype(jnp.bfloat16)
    grads = jnp.stack([grad_gate, grad_up])
    grads = lax.all_to_all(grads, "dp", split_axis=2, concat_axis=1, tiled=True)
    columns = lax.all_to_all(tokens_in, "tensor", split_axis=1, concat_axis=0, tiled=True)
    partial_xp = jnp.dot(columns, projector, preferred_element_type=jnp.float32)
    own_rows = lax.psum_scatter(partial_xp, "tensor", scatter_dimension=0, tiled=True).astype(
        jnp.bfloat16
    )
    xp = lax.all_gather(own_rows, ("dp", "tensor"), axis=0, tiled=True)
    contract = (((0,), (0,)), ((), ()))
    halves = [
        lax.dot_general(grads[k], xp, contract, preferred_element_type=jnp.float32) for k in (0, 1)
    ]
    summed = jnp.concatenate(halves, axis=1)
    return finish(summed, xp.shape[0], moment_m, moment_v)


def solution(mesh):
    return jax.shard_map(
        local,
        mesh=mesh,
        in_specs=(
            P(("dp", "tensor"), None),
            P("tensor", None),
            P("dp", "tensor"),
            P("dp", "tensor"),
            P("dp", "tensor"),
            P(("tensor", "dp"), None),
            P(("tensor", "dp"), None),
        ),
        out_specs=(P(("tensor", "dp"), None), P(("tensor", "dp"), None), P(("tensor", "dp"), None)),
        check_vma=False,
    )
```

time: 247 us -> 132 us (0.53)
  waiting for transfers between devices: 185 us -> 81.4 us
  blocking collectives: 22 us -> 0 us
  starting transfers between devices: 0.12 us -> 10.1 us
  matrix products: 12.8 us -> 3.87 us
  local copies, waits for them, and re-layouts: 6.92 us -> 12.7 us
  other arithmetic: 6.38 us -> 8.99 us
    reduce_scatter x2 -> x0, waiting for transfers between devices: 161 us -> none  [the longest x1 83.2 us: local(): lax.psum_scatter(lax.dot_general(grad_up, xp, contract, preferred_element...]
    all_gather x0 -> x1, waiting for transfers between devices: none -> 37.7 us  [local(): xp = lax.all_gather(own_rows, ('dp', 'tensor'), axis=0, tiled=True)]
    all_to_all x0 -> x2, waiting for transfers between devices: none -> 14.4 us  [the longest x1 14.4 us: local(): grads = lax.all_to_all(grads, 'dp', split_axis=2, concat_axis=1, tiled=True)]
    all_to_all x1 -> x0, blocking collectives: 13.5 us -> none  [local(): lax.all_to_all(tokens_in, 'tensor', split_axis=1, concat_axis=0, tiled=True)]
    all_to_all x0 -> x2, starting transfers between devices: none -> 10.1 us  [the longest x1 5.19 us: local(): lax.all_to_all(tokens_in, 'tensor', split_axis=1, concat_axis=0, tiled=True)]
    dot_general x2, matrix products: 11.6 us -> 2.71 us  [local(): lax.dot_general(grads[k], xp, contract, preferred_element_type=jnp.float32)]
    all_gather x1 -> x0, blocking collectives: 8.46 us -> none  [local(): xp = lax.all_gather(own_rows, 'tensor', axis=0, tiled=True)]
    another operation x0 -> x1, local copies, waits for them, and re-layouts: none -> 6.07 us  [local(): grads = jnp.stack([grad_gate, grad_up])]
  transfers between devices with their start and end apart: 3 -> 4, of which waited for: 3 -> 3; matrix products, arithmetic and copies ran while one was open for 3% -> 13% of each run, Pallas kernels for 0% -> 0%
where the time goes in v1:
time: 132 us; the launch traced here: 131 us
  waiting for transfers between devices  81.4 us (62%)
  between operations  14.1 us (11%)
  local copies, waits for them, and re-layouts  12.7 us (10%)
  starting transfers between devices  10.1 us (8%)
  other arithmetic  8.99 us (7%)
  matrix products  3.87 us (3%)
    all_gather x1, waiting for transfers between devices, local(): xp = lax.all_gather(own_rows, ('dp', 'tensor'), axis=0, tiled=True)  37.7 us
    reduce_scatter x1, waiting for transfers between devices, local(): lax.psum_scatter(partial_xp, 'tensor', scatter_dimension=0, tiled=True)  29.2 us
    all_to_all x1, waiting for transfers between devices, local(): grads = lax.all_to_all(grads, 'dp', split_axis=2, concat_axis=1, tiled=True)  14.4 us
    another operation x1, local copies, waits for them, and re-layouts, local(): grads = jnp.stack([grad_gate, grad_up])  6.07 us
    all_to_all x1, starting transfers between devices, local(): lax.all_to_all(tokens_in, 'tensor', split_axis=1, concat_axis=0, tiled=True)  5.19 us
    all_to_all x1, starting transfers between devices, local(): grads = lax.all_to_all(grads, 'dp', split_axis=2, concat_axis=1, tiled=True)  4.88 us
    another operation x2, other arithmetic, local(): grads = jnp.stack([grad_gate, grad_up])  4.25 us
    div x1, other arithmetic, finish(): direction = m_next / (jnp.sqrt(v_next) + 1e-08)  3.27 us
  transfers between devices with their start and end apart: 4, of which 3 were waited for; matrix products, arithmetic and copies ran while one was open for 13% of the time, Pallas kernels for 0%

profile of v1, /device:TPU:0, one launch (start us, length us, event | category | flops | bytes accessed | tf_op | source)
XLA Modules:
  0.0 131.2 jit_solution(9053729371313544651)
XLA Ops:
  7.2 0.0 copy-start
  7.2 2.0 %copy.46 = bf16[4,4,8,2048]{3,2,0,1:T(8,128)(2,1)} copy(bf16[4,4,8,2048]{3,2,1,0:T(8,128)(2,1)} %bitcast.36) | data formatting | bytes 1048576 | tf_op jit(solution)/shard_map/all_to_all | solution.py:24
  9.2 5.2 %all-to-all-start.1 = ((bf16[32,4,2048]{2,0,1:T(8,128)(2,1)}), bf16[32,4,2048]{2,0,1:T(8,128)(2,1)S(1)}, u32[]{:S(2)}, u32[]{:S(2)}) async-start(bf16[32,4,2048]{2,0,1:T(8,128)(2,1)} %bitcast.31), calls=%async_computation.1 | async-start | bytes 1048576 | tf_op jit(solution)/shard_map/all_to_all | solution.py:24
  14.4 2.8 %fusion.16 = (bf16[1,128,3840]{2,1,0:T(8,128)(2,1)S(1)}, bf16[1,128,3840]{2,1,0:T(8,128)(2,1)S(1)}) fusion(bf16[128,3840]{1,0:T(8,128)(2,1)} %param.9, bf16[128,3840]{1,0:T(8,128)(2,1)} %param.10, bf16[128,3840]{1,0:T(8,128)(2,1)} %param.11), kind=kLoop, calls=%fused_computation.25 | loop fusion | flops 7864320 | bytes 4915200 | tf_op jit(solution)/shard_map/stack | solution.py:22
  17.2 1.4 %pad_maximum_fusion = bf16[2,128,3840]{2,1,0:T(8,128)(2,1)} fusion(bf16[1,128,3840]{2,1,0:T(8,128)(2,1)S(1)} %get-tuple-element.9, bf16[1,128,3840]{2,1,0:T(8,128)(2,1)S(1)} %get-tuple-element.8), kind=kLoop, calls=%fused_computation.13 | loop fusion | flops 983040 | bytes 3932160 | tf_op jit(solution)/shard_map/stack | solution.py:22
  18.7 6.1 %copy.29 = bf16[2,128,3840]{1,0,2:T(2,128)(2,1)} copy(bf16[2,128,3840]{2,1,0:T(8,128)(2,1)} %pad_maximum_fusion) | data formatting | bytes 3932160 | tf_op jit(solution)/shard_map/stack | solution.py:22
  24.7 4.9 %all-to-all-start = ((bf16[2,128,3840]{1,0,2:T(2,128)(2,1)}), bf16[2,128,3840]{1,0,2:T(2,128)(2,1)}, u32[]{:S(2)}, u32[]{:S(2)}) async-start(bf16[2,128,3840]{1,0,2:T(2,128)(2,1)} %copy.29), calls=%async_computation | async-start | bytes 3932160 | tf_op jit(solution)/shard_map/all_to_all | solution.py:23
  29.6 0.0 reduce-scatter.2.cloned.1.call-start
  29.7 1.2 fusion.18
  30.8 0.0 reduce-scatter.2.cloned.1.call-update
  30.8 0.0 all-gather.2.cloned.1.call-start
  30.9 29.2 %reduce-scatter.2.cloned.1.call-done = f32[32,512]{1,0:T(8,128)} async-done(((f32[128,512]{1,0:T(8,128)}), f32[32,512]{1,0:T(8,128)}) %reduce-scatter.2.cloned.1.call-update) | async-done | bytes 65552 | tf_op jit(solution)/shard_map/reduce_scatter | solution.py:26
  60.1 1.5 %convert_element_type.23 = bf16[32,512]{1,0:T(8,128)(2,1)} convert(f32[32,512]{1,0:T(8,128)} %reduce-scatter.2.cloned.1.call-done) | non-fusion elementwise | flops 16384 | bytes 98304 | tf_op jit(solution)/shard_map/convert_element_type | solution.py:26
  61.6 0.0 all-gather.2.cloned.1.call-update
  61.6 14.4 %all-to-all-done = bf16[2,128,3840]{1,0,2:T(2,128)(2,1)} async-done(((bf16[2,128,3840]{1,0,2:T(2,128)(2,1)}), bf16[2,128,3840]{1,0,2:T(2,128)(2,1)}, u32[]{:S(2)}, u32[]{:S(2)}) %all-to-all-start) | async-done | bytes 1966112 | tf_op jit(solution)/shard_map/all_to_all | solution.py:23
  76.0 1.8 %copy.30 = bf16[2,128,3840]{1,2,0:T(8,128)(2,1)S(1)} copy(bf16[2,128,3840]{1,0,2:T(2,128)(2,1)} %all-to-all-done) | data formatting | bytes 3932160 | tf_op jit(solution)/shard_map/all_to_all | solution.py:23
  77.8 0.1 fusion.17
  78.0 0.4 copy.31
  78.4 1.3 %copy.33 = bf16[1,8,128,480]{2,1,3,0:T(8,128)(2,1)} copy(bf16[1,8,128,480]{2,3,1,0:T(8,128)(2,1)S(1)} %get-tuple-element.7) | data formatting | bytes 1966080 | tf_op jit(solution)/shard_map/slice | solution.py:32
  79.7 37.7 %all-gather.2.cloned.1.call-done = bf16[1024,512]{1,0:T(8,128)(2,1)} async-done(((bf16[32,512]{1,0:T(8,128)(2,1)}), bf16[1024,512]{1,0:T(8,128)(2,1)}) %all-gather.2.cloned.1.call-update) | async-done | bytes 1048592 | tf_op jit(solution)/shard_map/all_gather | solution.py:29
  117.4 2.0 %fusion.12 = f32[480,512]{1,0:T(8,128)S(1)} fusion(bf16[1024,512]{1,0:T(8,128)(2,1)} %all-gather.2.cloned.1.call-done, bf16[60,8,8,128]{3,2,1,0:T(8,128)(2,1)S(1)} %bitcast.34), kind=kOutput, calls=%fused_computation.21 | convolution fusion | flops 503316480 | bytes 3014656 | tf_op jit(solution)/shard_map/dot_general | solution.py:32
  119.5 0.7 fusion.9
  120.2 0.9 copy-done.1
  121.1 3.3 %add_divide_fusion = (f32[480,1024]{1,0:T(8,128)}, f32[480,1024]{1,0:T(8,128)}, f32[480,1024]{1,0:T(8,128)}) fusion(f32[480,512]{1,0:T(8,128)S(1)} %fusion.9, f32[480,512]{1,0:T(8,128)S(1)} %fusion.12, f32[480,1024]{1,0:T(8,128)S(1)} %copy-done.1, f32[480,1024]{1,0:T(8,128)S(1)} %copy-done.2), kind=kLoop, calls=%fused_computation.15 | loop fusion | flops 5406720 | bytes 11796480 | tf_op jit(solution)/shard_map/div | solution.py:11
  (9 shorter events, 0.0 us)
Async XLA Ops:
  7.2 22.5 %copy-start = (bf16[2048,512]{1,0:T(8,128)(2,1)S(1)}, bf16[2048,512]{1,0:T(8,128)(2,1)}, u32[]{:S(2)}) copy-start(bf16[2048,512]{1,0:T(8,128)(2,1)} %param.8) | copy-start | bytes 6291460
  9.2 15.5 %all-to-all-start.1 = ((bf16[32,4,2048]{2,0,1:T(8,128)(2,1)}), bf16[32,4,2048]{2,0,1:T(8,128)(2,1)S(1)}, u32[]{:S(2)}, u32[]{:S(2)}) async-start(bf16[32,4,2048]{2,0,1:T(8,128)(2,1)} %bitcast.31), calls=%async_computation.1 | async-start | bytes 1048576 | tf_op jit(solution)/shard_map/all_to_all | solution.py:24
  24.7 51.3 %all-to-all-start = ((bf16[2,128,3840]{1,0,2:T(2,128)(2,1)}), bf16[2,128,3840]{1,0,2:T(2,128)(2,1)}, u32[]{:S(2)}, u32[]{:S(2)}) async-start(bf16[2,128,3840]{1,0,2:T(2,128)(2,1)} %copy.29), calls=%async_computation | async-start | bytes 3932160 | tf_op jit(solution)/shard_map/all_to_all | solution.py:23
  29.6 30.5 %reduce-scatter.2.cloned.1.call-start = ((), (), s32[]{:S(2)}) async-start(), calls=%async_computation.3 | async-start | bytes 327680 | tf_op jit(solution)/shard_map/reduce_scatter | solution.py:26
  30.8 86.6 %all-gather.2.cloned.1.call-start = ((), (), s32[]{:S(2)}) async-start(), calls=%async_computation.4 | async-start | bytes 1081344 | tf_op jit(solution)/shard_map/all_gather | solution.py:29
  117.4 2.1 %copy-start.3 = (bf16[1,8,128,480]{2,1,3,0:T(8,128)(2,1)S(1)}, bf16[1,8,128,480]{2,1,3,0:T(8,128)(2,1)}, u32[]{:S(2)}) copy-start(bf16[1,8,128,480]{2,1,3,0:T(8,128)(2,1)} %copy.33) | copy-start | bytes 2949124
  117.4 2.1 %copy-start.4 = (bf16[1024,512]{1,0:T(8,128)(2,1)S(1)}, bf16[1024,512]{1,0:T(8,128)(2,1)}, u32[]{:S(2)}) copy-start(bf16[1024,512]{1,0:T(8,128)(2,1)} %all-gather.2.cloned.1.call-done) | copy-start | bytes 3145732
  117.4 2.8 %copy-start.2 = (f32[480,1024]{1,0:T(8,128)S(1)}, f32[480,1024]{1,0:T(8,128)}, u32[]{:S(2)}) copy-start(f32[480,1024]{1,0:T(8,128)} %param.12) | copy-start | bytes 5898244
  119.5 1.7 %copy-start.1 = (f32[480,1024]{1,0:T(8,128)S(1)}, f32[480,1024]{1,0:T(8,128)}, u32[]{:S(2)}) copy-start(f32[480,1024]{1,0:T(8,128)} %param.13) | copy-start | bytes 5898244
Sparse Core Ops, SparseCore 0:
  33.7 26.3 reduce-scatter.1
  63.7 53.6 all-gather.1

commit v2 on v1

--- a/solution.py
+++ b/solution.py
@@ -1,7 +1,302 @@
+import functools
+
 import jax
 import jax.numpy as jnp
 from jax import lax
+from jax.experimental import pallas as pl
+from jax.experimental.pallas import tpu as pltpu
 from jax.sharding import PartitionSpec as P
+
+
+MESH = pl.DeviceIdType.MESH
+
+
+def exchange_kernel(
+    ndp, nt, tok_ref, prj_ref, gate_ref, up_ref, hg_ref, out_ref,
+    g_v, u_v, h_v, prj_v, cols, part, rs_buf, xp_all, grads, recv,
+    load_sem, tok_send, tok_recv, rs_send, rs_recv,
+    xz_send, xt_send, xc_send, xp_recv, xc_recv, g_send, g_recv,
+):
+    d = lax.axis_index("dp")
+    t = lax.axis_index("tensor")
+    nz = ndp // 2
+    z, c = d // 2, d % 2
+    sub = tok_ref.shape[0]
+    grp = sub * nt
+    dcol = tok_ref.shape[1] // nt
+    rows = recv.shape[2]
+    rank = prj_ref.shape[1]
+    half = ndp // 2
+    half_tiles = half * rows // 128
+
+    barrier = pltpu.get_barrier_semaphore()
+    for k in range(1, ndp):
+        pl.semaphore_signal(barrier, inc=1, device_id=((d + k) % ndp, t), device_id_type=MESH)
+    for k in range(1, nt):
+        pl.semaphore_signal(barrier, inc=1, device_id=(d, (t + k) % nt), device_id_type=MESH)
+
+    loads = [
+        pltpu.make_async_copy(src, dst, load_sem.at[i])
+        for i, (src, dst) in enumerate(
+            ((gate_ref, g_v), (up_ref, u_v), (hg_ref, h_v), (prj_ref, prj_v))
+        )
+    ]
+    own_tok = pltpu.make_async_copy(
+        tok_ref.at[:, pl.ds(pl.multiple_of(t * dcol, 128), dcol)],
+        cols.at[pl.ds(pl.multiple_of(t * sub, 16), sub), :],
+        load_sem.at[4],
+    )
+    for load in loads:
+        load.start()
+    own_tok.start()
+    pl.semaphore_wait(barrier, ndp + nt - 2)
+
+    def tok_copy(dest, src):
+        return pltpu.make_async_remote_copy(
+            src_ref=tok_ref.at[:, pl.ds(pl.multiple_of(dest * dcol, 128), dcol)],
+            dst_ref=cols.at[pl.ds(pl.multiple_of(src * sub, 16), sub), :],
+            send_sem=tok_send.at[dest],
+            recv_sem=tok_recv.at[src],
+            device_id=(d, dest),
+            device_id_type=MESH,
+        )
+
+    for k in range(1, nt):
+        tok_copy((t + k) % nt, t).start()
+
+    for load in loads[:3]:
+        load.wait()
+
+    def tile(i, carry):
+        at = pl.ds(pl.multiple_of(i * 128, 128), 128)
+        gate = g_v[:, at].astype(jnp.float32)
+        upval = u_v[:, at].astype(jnp.float32)
+        hgrad = h_v[:, at].astype(jnp.float32)
+        sig = jax.nn.sigmoid(gate)
+        grad_gate = hgrad * upval * sig * (1.0 + gate * (1.0 - sig))
+        grad_up = hgrad * gate * sig
+        grads[0, at, :] = grad_gate.astype(jnp.bfloat16).T
+        grads[1, at, :] = grad_up.astype(jnp.bfloat16).T
+        return carry
+
+    def block_of(dest):
+        return grads.at[:, pl.ds(pl.multiple_of(dest * rows, 16), rows), :]
+
+    def grad_copy(dest, src):
+        return pltpu.make_async_remote_copy(
+            src_ref=block_of(dest),
+            dst_ref=recv.at[src],
+            send_sem=g_send.at[dest],
+            recv_sem=g_recv.at[src],
+            device_id=(dest, t),
+            device_id_type=MESH,
+        )
+
+    own_grad = pltpu.make_async_copy(block_of(d), recv.at[d], load_sem.at[5])
+
+    own_half = d // half
+    inner = (z * (nz - 1 - z) + nz * nz - 1) // (nz * nz)
+    first = own_half * (1 - inner) + (1 - own_half) * inner
+
+    def send_block(dest):
+        @pl.when(dest != d)
+        def _():
+            grad_copy(dest, d).start()
+
+        @pl.when(dest == d)
+        def _():
+            own_grad.start()
+
+    def tiles_of(which, start, stop):
+        lax.fori_loop(which * half_tiles + start, which * half_tiles + stop, tile, 0)
+
+    done = 0
+    for j in range(half):
+        need = -(-((j + 1) * rows) // 128)
+        tiles_of(first, done, need)
+        done = need
+        send_block(first * half + j)
+    tiles_of(1 - first, 0, half_tiles)
+
+    loads[3].wait()
+    own_tok.wait()
+    for k in range(1, nt):
+        tok_copy(t, (t + k) % nt).wait_recv()
+    part[...] = jnp.dot(cols[...], prj_v[...], preferred_element_type=jnp.float32)
+
+    def rs_copy(dest, src):
+        return pltpu.make_async_remote_copy(
+            src_ref=part.at[pl.ds(pl.multiple_of(dest * sub, 16), sub), :],
+            dst_ref=rs_buf.at[src],
+            send_sem=rs_send.at[dest],
+            recv_sem=rs_recv.at[src],
+            device_id=(d, dest),
+            device_id_type=MESH,
+        )
+
+    for k in range(1, nt):
+        rs_copy((t + k) % nt, t).start()
+    rs_buf[t] = part[pl.ds(pl.multiple_of(t * sub, 16), sub), :]
+    for k in range(1, nt):
+        rs_copy(t, (t + k) % nt).wait_recv()
+    total = rs_buf[0]
+    for k in range(1, nt):
+        total = total + rs_buf[k]
+
+    def piece(dd, tt):
+        return xp_all.at[pl.ds(pl.multiple_of(dd * grp + tt * sub, 16), sub), :]
+
+    xp_all[pl.ds(pl.multiple_of(d * grp + t * sub, 16), sub), :] = total.astype(jnp.bfloat16)
+
+    def piece_copy(dd, tt, send_sem, dest):
+        return pltpu.make_async_remote_copy(
+            src_ref=piece(dd, tt),
+            dst_ref=piece(dd, tt),
+            send_sem=send_sem,
+            recv_sem=xp_recv.at[dd * nt + tt],
+            device_id=dest,
+            device_id_type=MESH,
+        )
+
+    for k in range(1, nz):
+        zz = (z + k) % nz
+        piece_copy(d, t, xz_send.at[zz], (zz * 2 + c, t)).start()
+
+    for j in range(half):
+        send_block((1 - first) * half + j)
+
+    if nz == 4:
+        order = [z, z + 1 - 2 * (z % 2), 2 - z // 2, 3 - 3 * (z // 2)]
+    else:
+        order = [(z + k) % nz for k in range(nz)]
+
+    for k, zz in enumerate(order):
+        dd = zz * 2 + c
+        if k:
+            piece_copy(dd, t, xz_send.at[zz], (dd, t)).wait_recv()
+        for kt in range(1, nt):
+            tt = (t + kt) % nt
+            piece_copy(dd, t, xt_send.at[zz * nt + tt], (d, tt)).start()
+
+    partner = d + 1 - 2 * c
+
+    def core_copy(zz, parity):
+        group = xp_all.at[pl.ds(pl.multiple_of((zz * 2 + parity) * grp, 128), grp), :]
+        return pltpu.make_async_remote_copy(
+            src_ref=group,
+            dst_ref=group,
+            send_sem=xc_send.at[zz],
+            recv_sem=xc_recv.at[zz],
+            device_id=(partner, t),
+            device_id_type=MESH,
+        )
+
+    for zz in order:
+        for kt in range(1, nt):
+            tt = (t + kt) % nt
+            piece_copy(zz * 2 + c, tt, xt_send.at[zz * nt + tt], (d, tt)).wait_recv()
+        core_copy(zz, c).start()
+
+    for k, zz in enumerate(order):
+        core_copy(zz, 1 - c).wait_recv()
+        if k == 0:
+            own_grad.wait()
+            grad_copy(d, partner).wait_recv()
+        else:
+            grad_copy(d, zz * 2).wait_recv()
+            grad_copy(d, zz * 2 + 1).wait_recv()
+        xp = xp_all[pl.ds(pl.multiple_of(zz * 2 * grp, 128), 2 * grp), :]
+        for part_of in (0, 1):
+            lhs = jnp.concatenate([recv[zz * 2, part_of], recv[zz * 2 + 1, part_of]], axis=1)
+            term = jnp.dot(lhs, xp, preferred_element_type=jnp.float32)
+            at = slice(part_of * rank, (part_of + 1) * rank)
+            if k == 0:
+                out_ref[:, at] = term
+            else:
+                out_ref[:, at] += term
+
+    for k in range(1, nt):
+        dest = (t + k) % nt
+        tok_copy(dest, t).wait_send()
+        rs_copy(dest, t).wait_send()
+        for zz in range(nz):
+            piece_copy(zz * 2 + c, t, xt_send.at[zz * nt + dest], (d, dest)).wait_send()
+    for k in range(1, nz):
+        zz = (z + k) % nz
+        piece_copy(d, t, xz_send.at[zz], (zz * 2 + c, t)).wait_send()
+    for zz in range(nz):
+        core_copy(zz, c).wait_send()
+    for k in range(1, ndp):
+        grad_copy((d + k) % ndp, d).wait_send()
+
+
+def exchange(ndp, nt, tokens_in, projector, gate_pre, up_pre, hidden_grad):
+    sub, width = tokens_in.shape
+    depth, rank = projector.shape
+    grp, cols = gate_pre.shape
+    rows = cols // ndp
+    dma = pltpu.SemaphoreType.DMA
+    bf, f32 = jnp.bfloat16, jnp.float32
+    nz = ndp // 2
+    flops = 2 * grp * depth * rank + 4 * rows * grp * ndp * rank
+    return pl.pallas_call(
+        functools.partial(exchange_kernel, ndp, nt),
+        out_shape=jax.ShapeDtypeStruct((rows, 2 * rank), f32),
+        in_specs=[pl.BlockSpec(memory_space=pl.ANY)] * 5,
+        out_specs=pl.BlockSpec(memory_space=pltpu.VMEM),
+        scratch_shapes=[
+            pltpu.VMEM((grp, cols), bf),
+            pltpu.VMEM((grp, cols), bf),
+            pltpu.VMEM((grp, cols), bf),
+            pltpu.VMEM((depth, rank), bf),
+            pltpu.VMEM((grp, depth), bf),
+            pltpu.VMEM((grp, rank), f32),
+            pltpu.VMEM((nt, sub, rank), f32),
+            pltpu.VMEM((grp * ndp, rank), bf),
+            pltpu.VMEM((2, cols, grp), bf),
+            pltpu.VMEM((ndp, 2, rows, grp), bf),
+            dma((6,)),
+            dma((nt,)),
+            dma((nt,)),
+            dma((nt,)),
+            dma((nt,)),
+            dma((nz,)),
+            dma((nz * nt,)),
+            dma((nz,)),
+            dma((ndp * nt,)),
+            dma((nz,)),
+            dma((ndp,)),
+            dma((ndp,)),
+        ],
+        compiler_params=pltpu.CompilerParams(
+            collective_id=0, has_side_effects=True, vmem_limit_bytes=32 * 1024 * 1024
+        ),
+        cost_estimate=pl.CostEstimate(
+            flops=flops, bytes_accessed=8 * grp * cols, transcendentals=grp * cols
+        ),
+    )(tokens_in, projector, gate_pre, up_pre, hidden_grad)
+
+
+def fits(ndp, nt, tokens_in, projector, gate_pre):
+    sub, width = tokens_in.shape
+    grp, cols = gate_pre.shape
+    return (
+        ndp % 2 == 0
+        and ndp >= 4
+        and nt >= 2
+        and grp == 128
+        and sub * nt == grp
+        and sub % 16 == 0
+        and cols % ndp == 0
+        and (cols // ndp) % 16 == 0
+        and cols % 256 == 0
+        and width % (128 * nt) == 0
+        and projector.shape[0] == width // nt
+        and projector.shape[1] % 128 == 0
+        and cols <= 8192
+        and projector.size <= 2**21
+        and grp * ndp <= 4096
+    )
 
 
 def finish(summed, total_tokens, moment_m, moment_v):
@@ -13,6 +308,10 @@
 
 
 def local(tokens_in, projector, gate_pre, up_pre, hidden_grad, moment_m, moment_v):
+    ndp, nt = lax.axis_size("dp"), lax.axis_size("tensor")
+    if fits(ndp, nt, tokens_in, projector, gate_pre):
+        summed = exchange(ndp, nt, tokens_in, projector, gate_pre, up_pre, hidden_grad)
+        return finish(summed, gate_pre.shape[0] * ndp, moment_m, moment_v)
     gate = gate_pre.astype(jnp.float32)
     hgrad = hidden_grad.astype(jnp.float32)
     sig = jax.nn.sigmoid(gate)

time: 132 us -> 69.7 us (0.53)
  waiting for transfers between devices: 81.4 us -> 0 us
  Pallas kernels: 0 us -> 58.9 us
  between operations: 14.1 us -> 0.67 us
  starting transfers between devices: 10.1 us -> 0 us
  local copies, waits for them, and re-layouts: 12.7 us -> 6.24 us
  other arithmetic: 8.99 us -> 3.61 us
  matrix products: 3.87 us -> 0 us
    pallas_call x0 -> x1, Pallas kernels: none -> 58.9 us  [exchange(): pl.pallas_call(functools.partial(exchange_kernel, ndp, nt), out_shape=jax...]
    all_gather x1 -> x0, waiting for transfers between devices: 37.7 us -> none  [local(): xp = lax.all_gather(own_rows, ('dp', 'tensor'), axis=0, tiled=True)]
    reduce_scatter x1 -> x0, waiting for transfers between devices: 29.2 us -> none  [local(): lax.psum_scatter(partial_xp, 'tensor', scatter_dimension=0, tiled=True)]
    all_to_all x2 -> x0, waiting for transfers between devices: 14.4 us -> none  [the longest x1 14.4 us: local(): grads = lax.all_to_all(grads, 'dp', split_axis=2, concat_axis=1, tiled=True)]
    all_to_all x2 -> x0, starting transfers between devices: 10.1 us -> none  [the longest x1 5.19 us: local(): lax.all_to_all(tokens_in, 'tensor', split_axis=1, concat_axis=0, tiled=True)]
    another operation x1 -> x0, local copies, waits for them, and re-layouts: 6.07 us -> none  [local(): grads = jnp.stack([grad_gate, grad_up])]
    unnamed x10 -> x14, local copies, waits for them, and re-layouts: 0.97 us -> 6.24 us
    another operation x2 -> x0, other arithmetic: 4.25 us -> none  [local(): grads = jnp.stack([grad_gate, grad_up])]
  transfers between devices with their start and end apart: 4 -> 0, of which waited for: 3 -> 0; matrix products, arithmetic and copies ran while one was open for 13% -> 0% of each run, Pallas kernels for 0% -> 0%
where the time goes in v2:
time: 69.7 us; the launch traced here: 69.4 us
  Pallas kernels  58.9 us (85%)
  local copies, waits for them, and re-layouts  6.24 us (9%)
  other arithmetic  3.61 us (5%)
    pallas_call x1, Pallas kernels, exchange(): pl.pallas_call(functools.partial(exchange_kernel, ndp, nt), out_shape=jax...  58.9 us
    unnamed x14, local copies, waits for them, and re-layouts  6.24 us
    div x1, other arithmetic, finish(): direction = m_next / (jnp.sqrt(v_next) + 1e-08)  3.61 us

profile of v2, /device:TPU:0, one launch (start us, length us, event | category | flops | bytes accessed | tf_op | source)
XLA Modules:
  0.0 69.4 jit_solution(8733660573763345957)
XLA Ops:
  0.6 0.0 copy-start
  0.6 1.6 %copy-done = bf16[2048,512]{1,0:T(8,128)(2,1)S(1)} copy-done((bf16[2048,512]{1,0:T(8,128)(2,1)S(1)}, bf16[2048,512]{1,0:T(8,128)(2,1)}, u32[]{:S(2)}) %copy-start) | copy-done | bytes 2097176
  2.2 0.0 copy-start.1
  2.2 1.2 %copy-done.1 = bf16[128,3840]{1,0:T(8,128)(2,1)S(1)} copy-done((bf16[128,3840]{1,0:T(8,128)(2,1)S(1)}, bf16[128,3840]{1,0:T(8,128)(2,1)}, u32[]{:S(2)}) %copy-start.1) | copy-done | bytes 983064
  3.4 0.0 copy-start.2
  3.4 1.2 %copy-done.2 = bf16[128,3840]{1,0:T(8,128)(2,1)S(1)} copy-done((bf16[128,3840]{1,0:T(8,128)(2,1)S(1)}, bf16[128,3840]{1,0:T(8,128)(2,1)}, u32[]{:S(2)}) %copy-start.2) | copy-done | bytes 983064
  4.6 0.0 copy-start.3
  4.6 1.2 %copy-done.3 = bf16[128,3840]{1,0:T(8,128)(2,1)S(1)} copy-done((bf16[128,3840]{1,0:T(8,128)(2,1)S(1)}, bf16[128,3840]{1,0:T(8,128)(2,1)}, u32[]{:S(2)}) %copy-start.3) | copy-done | bytes 983064
  5.8 0.0 copy-start.4
  5.8 1.0 %copy-done.4 = bf16[32,8192]{1,0:T(8,128)(2,1)S(1)} copy-done((bf16[32,8192]{1,0:T(8,128)(2,1)S(1)}, bf16[32,8192]{1,0:T(8,128)(2,1)}, u32[]{:S(2)}) %copy-start.4) | copy-done | bytes 524312
  6.9 0.0 copy-start.5
  6.9 0.0 copy-start.6
  6.9 58.9 %shard_map.94 = f32[480,1024]{1,0:T(8,128)S(1)} custom-call(bf16[32,8192]{1,0:T(8,128)(2,1)S(1)} %copy-done.4, bf16[2048,512]{1,0:T(8,128)(2,1)S(1)} %copy-done, bf16[128,3840]{1,0:T(8,128)(2,1)S(1)} %copy-done.1, bf16[128,3840]{1,0:T(8,128)(2,1)S(1)} %copy-done.2, bf16[128,3840]{1,0:T(8,128)(2,1)S(1)} %copy-done.3), custom_call_target="tpu_custom_call" | custom-call | flops 1275068416 | bytes 3932160 | tf_op jit(solution)/shard_map/pallas_call | solution.py:242
  65.8 0.0 copy-done.5
  65.8 0.0 copy-done.6
  65.8 3.6 %add_divide_fusion = (f32[480,1024]{1,0:T(8,128)}, f32[480,1024]{1,0:T(8,128)}, f32[480,1024]{1,0:T(8,128)}) fusion(f32[480,1024]{1,0:T(8,128)S(1)} %shard_map.94, f32[480,1024]{1,0:T(8,128)S(1)} %copy-done.5, f32[480,1024]{1,0:T(8,128)S(1)} %copy-done.6), kind=kLoop, calls=%fused_computation | loop fusion | flops 4915200 | bytes 11796480 | tf_op jit(solution)/shard_map/div | solution.py:306
Async XLA Ops:
  0.6 1.6 %copy-start = (bf16[2048,512]{1,0:T(8,128)(2,1)S(1)}, bf16[2048,512]{1,0:T(8,128)(2,1)}, u32[]{:S(2)}) copy-start(bf16[2048,512]{1,0:T(8,128)(2,1)} %prj_ref.1) | copy-start | bytes 6291460
  2.2 1.2 %copy-start.1 = (bf16[128,3840]{1,0:T(8,128)(2,1)S(1)}, bf16[128,3840]{1,0:T(8,128)(2,1)}, u32[]{:S(2)}) copy-start(bf16[128,3840]{1,0:T(8,128)(2,1)} %gate_ref.1) | copy-start | bytes 2949124
  3.4 1.2 %copy-start.2 = (bf16[128,3840]{1,0:T(8,128)(2,1)S(1)}, bf16[128,3840]{1,0:T(8,128)(2,1)}, u32[]{:S(2)}) copy-start(bf16[128,3840]{1,0:T(8,128)(2,1)} %up_ref.1) | copy-start | bytes 2949124
  4.6 1.2 %copy-start.3 = (bf16[128,3840]{1,0:T(8,128)(2,1)S(1)}, bf16[128,3840]{1,0:T(8,128)(2,1)}, u32[]{:S(2)}) copy-start(bf16[128,3840]{1,0:T(8,128)(2,1)} %hg_ref.1) | copy-start | bytes 2949124
  5.8 1.0 %copy-start.4 = (bf16[32,8192]{1,0:T(8,128)(2,1)S(1)}, bf16[32,8192]{1,0:T(8,128)(2,1)}, u32[]{:S(2)}) copy-start(bf16[32,8192]{1,0:T(8,128)(2,1)} %tok_ref.1) | copy-start | bytes 1572868
  6.9 58.9 %copy-start.5 = (f32[480,1024]{1,0:T(8,128)S(1)}, f32[480,1024]{1,0:T(8,128)}, u32[]{:S(2)}) copy-start(f32[480,1024]{1,0:T(8,128)} %param.13) | copy-start | bytes 5898244
  6.9 58.9 %copy-start.6 = (f32[480,1024]{1,0:T(8,128)S(1)}, f32[480,1024]{1,0:T(8,128)}, u32[]{:S(2)}) copy-start(f32[480,1024]{1,0:T(8,128)} %param.12) | copy-start | bytes 5898244

commit v3 on v2

--- a/solution.py
+++ b/solution.py
@@ -29,27 +29,42 @@
     half = ndp // 2
     half_tiles = half * rows // 128
 
+    own_half = d // half
+    inner = (z * (nz - 1 - z) + nz * nz - 1) // (nz * nz)
+    first = own_half * (1 - inner) + (1 - own_half) * inner
+
+    head = -(-rows // 128)
+    spans = (
+        (first * half_tiles, head),
+        (first * half_tiles + head, half_tiles - head),
+        ((1 - first) * half_tiles, half_tiles),
+    )
+    loads = []
+    for i, (start, count) in enumerate(spans):
+        at = pl.ds(pl.multiple_of(start * 128, 128), count * 128)
+        for k, (src, dst) in enumerate(((gate_ref, g_v), (up_ref, u_v), (hg_ref, h_v))):
+            loads.append(
+                pltpu.make_async_copy(src.at[:, at], dst.at[:, at], load_sem.at[3 * i + k])
+            )
+    load_prj = pltpu.make_async_copy(prj_ref, prj_v, load_sem.at[9])
+    own_tok = pltpu.make_async_copy(
+        tok_ref.at[:, pl.ds(pl.multiple_of(t * dcol, 128), dcol)],
+        cols.at[pl.ds(pl.multiple_of(t * sub, 16), sub), :],
+        load_sem.at[10],
+    )
+    for load in loads[:3]:
+        load.start()
+
     barrier = pltpu.get_barrier_semaphore()
     for k in range(1, ndp):
         pl.semaphore_signal(barrier, inc=1, device_id=((d + k) % ndp, t), device_id_type=MESH)
     for k in range(1, nt):
         pl.semaphore_signal(barrier, inc=1, device_id=(d, (t + k) % nt), device_id_type=MESH)
 
-    loads = [
-        pltpu.make_async_copy(src, dst, load_sem.at[i])
-        for i, (src, dst) in enumerate(
-            ((gate_ref, g_v), (up_ref, u_v), (hg_ref, h_v), (prj_ref, prj_v))
-        )
-    ]
-    own_tok = pltpu.make_async_copy(
-        tok_ref.at[:, pl.ds(pl.multiple_of(t * dcol, 128), dcol)],
-        cols.at[pl.ds(pl.multiple_of(t * sub, 16), sub), :],
-        load_sem.at[4],
-    )
-    for load in loads:
+    for load in loads[3:]:
         load.start()
+    load_prj.start()
     own_tok.start()
-    pl.semaphore_wait(barrier, ndp + nt - 2)
 
     def tok_copy(dest, src):
         return pltpu.make_async_remote_copy(
@@ -60,12 +75,6 @@
             device_id=(d, dest),
             device_id_type=MESH,
         )
-
-    for k in range(1, nt):
-        tok_copy((t + k) % nt, t).start()
-
-    for load in loads[:3]:
-        load.wait()
 
     def tile(i, carry):
         at = pl.ds(pl.multiple_of(i * 128, 128), 128)
@@ -92,11 +101,7 @@
             device_id_type=MESH,
         )
 
-    own_grad = pltpu.make_async_copy(block_of(d), recv.at[d], load_sem.at[5])
-
-    own_half = d // half
-    inner = (z * (nz - 1 - z) + nz * nz - 1) // (nz * nz)
-    first = own_half * (1 - inner) + (1 - own_half) * inner
+    own_grad = pltpu.make_async_copy(block_of(d), recv.at[d], load_sem.at[11])
 
     def send_block(dest):
         @pl.when(dest != d)
@@ -110,15 +115,27 @@
     def tiles_of(which, start, stop):
         lax.fori_loop(which * half_tiles + start, which * half_tiles + stop, tile, 0)
 
-    done = 0
-    for j in range(half):
+    for load in loads[:3]:
+        load.wait()
+    tiles_of(first, 0, head)
+    pl.semaphore_wait(barrier, ndp + nt - 2)
+    send_block(first * half)
+    for k in range(1, nt):
+        tok_copy((t + k) % nt, t).start()
+
+    for load in loads[3:6]:
+        load.wait()
+    done = head
+    for j in range(1, half):
         need = -(-((j + 1) * rows) // 128)
         tiles_of(first, done, need)
         done = need
         send_block(first * half + j)
+    for load in loads[6:]:
+        load.wait()
     tiles_of(1 - first, 0, half_tiles)
 
-    loads[3].wait()
+    load_prj.wait()
     own_tok.wait()
     for k in range(1, nt):
         tok_copy(t, (t + k) % nt).wait_recv()
@@ -238,11 +255,12 @@
     dma = pltpu.SemaphoreType.DMA
     bf, f32 = jnp.bfloat16, jnp.float32
     nz = ndp // 2
+    operands = (tokens_in, projector, gate_pre, up_pre, hidden_grad)
     flops = 2 * grp * depth * rank + 4 * rows * grp * ndp * rank
     return pl.pallas_call(
         functools.partial(exchange_kernel, ndp, nt),
         out_shape=jax.ShapeDtypeStruct((rows, 2 * rank), f32),
-        in_specs=[pl.BlockSpec(memory_space=pl.ANY)] * 5,
+        in_specs=[pl.BlockSpec(memory_space=pltpu.HBM)] * 5,
         out_specs=pl.BlockSpec(memory_space=pltpu.VMEM),
         scratch_shapes=[
             pltpu.VMEM((grp, cols), bf),
@@ -255,7 +273,7 @@
             pltpu.VMEM((grp * ndp, rank), bf),
             pltpu.VMEM((2, cols, grp), bf),
             pltpu.VMEM((ndp, 2, rows, grp), bf),
-            dma((6,)),
+            dma((12,)),
             dma((nt,)),
             dma((nt,)),
             dma((nt,)),
@@ -274,7 +292,7 @@
         cost_estimate=pl.CostEstimate(
             flops=flops, bytes_accessed=8 * grp * cols, transcendentals=grp * cols
         ),
-    )(tokens_in, projector, gate_pre, up_pre, hidden_grad)
+    )(*[pltpu.with_memory_space_constraint(x, pltpu.HBM) for x in operands])
 
 
 def fits(ndp, nt, tokens_in, projector, gate_pre):

time: 69.7 us -> 63.1 us (0.905)
  local copies, waits for them, and re-layouts: 6.24 us -> 0.01 us
    unnamed x14 -> x4, local copies, waits for them, and re-layouts: 6.24 us -> 0.01 us
where the time goes in v3:
time: 63.1 us; the launch traced here: 63 us
  Pallas kernels  58.7 us (93%)
  other arithmetic  3.61 us (6%)
  between operations  0.67 us (1%)
    pallas_call x1, Pallas kernels, exchange(): pl.pallas_call(functools.partial(exchange_kernel, ndp, nt), out_shape=jax...  58.7 us
    div x1, other arithmetic, finish(): direction = m_next / (jnp.sqrt(v_next) + 1e-08)  3.61 us

profile of v3, /device:TPU:0, one launch (start us, length us, event | category | flops | bytes accessed | tf_op | source)
XLA Modules:
  0.0 63.0 jit_solution(16502477249785579111)
XLA Ops:
  0.6 0.0 copy-start
  0.6 0.0 copy-start.1
  0.7 58.7 %shard_map.94 = f32[480,1024]{1,0:T(8,128)S(1)} custom-call(bf16[32,8192]{1,0:T(8,128)(2,1)} %tok_ref.1, bf16[2048,512]{1,0:T(8,128)(2,1)} %prj_ref.1, bf16[128,3840]{1,0:T(8,128)(2,1)} %gate_ref.1, bf16[128,3840]{1,0:T(8,128)(2,1)} %up_ref.1, bf16[128,3840]{1,0:T(8,128)(2,1)} %hg_ref.1), custom_call_target="tpu_custom_call" | custom-call | flops 1275068416 | bytes 3932160 | tf_op jit(solution)/shard_map/pallas_call | solution.py:260
  59.4 0.0 copy-done
  59.4 0.0 copy-done.1
  59.4 3.6 %add_divide_fusion = (f32[480,1024]{1,0:T(8,128)}, f32[480,1024]{1,0:T(8,128)}, f32[480,1024]{1,0:T(8,128)}) fusion(f32[480,1024]{1,0:T(8,128)S(1)} %shard_map.94, f32[480,1024]{1,0:T(8,128)S(1)} %copy-done, f32[480,1024]{1,0:T(8,128)S(1)} %copy-done.1), kind=kLoop, calls=%fused_computation | loop fusion | flops 4915200 | bytes 11796480 | tf_op jit(solution)/shard_map/div | solution.py:324
Async XLA Ops:
  0.6 58.7 %copy-start = (f32[480,1024]{1,0:T(8,128)S(1)}, f32[480,1024]{1,0:T(8,128)}, u32[]{:S(2)}) copy-start(f32[480,1024]{1,0:T(8,128)} %param.13) | copy-start | bytes 5898244
  0.6 58.7 %copy-start.1 = (f32[480,1024]{1,0:T(8,128)S(1)}, f32[480,1024]{1,0:T(8,128)}, u32[]{:S(2)}) copy-start(f32[480,1024]{1,0:T(8,128)} %param.12) | copy-start | bytes 5898244

commit v4 on v3

--- a/solution.py
+++ b/solution.py
@@ -115,13 +115,13 @@
     def tiles_of(which, start, stop):
         lax.fori_loop(which * half_tiles + start, which * half_tiles + stop, tile, 0)
 
+    pl.semaphore_wait(barrier, ndp + nt - 2)
+    for k in range(1, nt):
+        tok_copy((t + k) % nt, t).start()
     for load in loads[:3]:
         load.wait()
     tiles_of(first, 0, head)
-    pl.semaphore_wait(barrier, ndp + nt - 2)
     send_block(first * half)
-    for k in range(1, nt):
-        tok_copy((t + k) % nt, t).start()
 
     for load in loads[3:6]:
         load.wait()
@@ -130,7 +130,10 @@
         need = -(-((j + 1) * rows) // 128)
         tiles_of(first, done, need)
         done = need
-        send_block(first * half + j)
+        if j < 2:
+            send_block(first * half + j)
+        else:
+            pl.when(inner == 0)(functools.partial(send_block, first * half + j))
     for load in loads[6:]:
         load.wait()
     tiles_of(1 - first, 0, half_tiles)
@@ -179,11 +182,13 @@
         zz = (z + k) % nz
         piece_copy(d, t, xz_send.at[zz], (zz * 2 + c, t)).start()
 
+    for j in range(2, half):
+        pl.when(inner == 1)(functools.partial(send_block, first * half + j))
     for j in range(half):
         send_block((1 - first) * half + j)
 
     if nz == 4:
-        order = [z, z + 1 - 2 * (z % 2), 2 - z // 2, 3 - 3 * (z // 2)]
+        order = [z, z + 1 - 2 * (z % 2), 3 - 3 * (z // 2), 2 - z // 2]
     else:
         order = [(z + k) % nz for k in range(nz)]
 

time: 63.1 us -> 57.1 us (0.905)
  the two profiles are of different devices: /device:TPU:0 before, /device:TPU:25 now
where the time goes in v4:
time: 57.1 us; the launch traced here: 57 us
  Pallas kernels  52.7 us (92%)
  other arithmetic  3.61 us (6%)
  between operations  0.67 us (1%)
    pallas_call x1, Pallas kernels, exchange(): pl.pallas_call(functools.partial(exchange_kernel, ndp, nt), out_shape=jax...  52.7 us
    div x1, other arithmetic, finish(): direction = m_next / (jnp.sqrt(v_next) + 1e-08)  3.61 us

profile of v4, /device:TPU:25, one launch (start us, length us, event | category | flops | bytes accessed | tf_op | source)
XLA Modules:
  0.0 57.0 jit_solution(5950301590225668543)
XLA Ops:
  0.6 0.0 copy-start
  0.6 0.0 copy-start.1
  0.7 52.7 %shard_map.94 = f32[480,1024]{1,0:T(8,128)S(1)} custom-call(bf16[32,8192]{1,0:T(8,128)(2,1)} %tok_ref.1, bf16[2048,512]{1,0:T(8,128)(2,1)} %prj_ref.1, bf16[128,3840]{1,0:T(8,128)(2,1)} %gate_ref.1, bf16[128,3840]{1,0:T(8,128)(2,1)} %up_ref.1, bf16[128,3840]{1,0:T(8,128)(2,1)} %hg_ref.1), custom_call_target="tpu_custom_call" | custom-call | flops 1275068416 | bytes 3932160 | tf_op jit(solution)/shard_map/pallas_call | solution.py:265
  53.3 0.0 copy-done
  53.3 0.0 copy-done.1
  53.3 3.6 %add_divide_fusion = (f32[480,1024]{1,0:T(8,128)}, f32[480,1024]{1,0:T(8,128)}, f32[480,1024]{1,0:T(8,128)}) fusion(f32[480,1024]{1,0:T(8,128)S(1)} %shard_map.94, f32[480,1024]{1,0:T(8,128)S(1)} %copy-done, f32[480,1024]{1,0:T(8,128)S(1)} %copy-done.1), kind=kLoop, calls=%fused_computation | loop fusion | flops 4915200 | bytes 11796480 | tf_op jit(solution)/shard_map/div | solution.py:329
Async XLA Ops:
  0.6 52.7 %copy-start = (f32[480,1024]{1,0:T(8,128)S(1)}, f32[480,1024]{1,0:T(8,128)}, u32[]{:S(2)}) copy-start(f32[480,1024]{1,0:T(8,128)} %param.13) | copy-start | bytes 5898244
  0.6 52.7 %copy-start.1 = (f32[480,1024]{1,0:T(8,128)S(1)}, f32[480,1024]{1,0:T(8,128)}, u32[]{:S(2)}) copy-start(f32[480,1024]{1,0:T(8,128)} %param.12) | copy-start | bytes 5898244

commit v5 on v4

--- a/solution.py
+++ b/solution.py
@@ -9,6 +9,7 @@
 
 
 MESH = pl.DeviceIdType.MESH
+HELD = 5
 
 
 def exchange_kernel(
@@ -88,29 +89,30 @@
         grads[1, at, :] = grad_up.astype(jnp.bfloat16).T
         return carry
 
-    def block_of(dest):
-        return grads.at[:, pl.ds(pl.multiple_of(dest * rows, 16), rows), :]
-
-    def grad_copy(dest, src):
+    def block_of(dest, side):
+        return grads.at[side, pl.ds(pl.multiple_of(dest * rows, 16), rows), :]
+
+    def grad_copy(dest, src, side):
         return pltpu.make_async_remote_copy(
-            src_ref=block_of(dest),
-            dst_ref=recv.at[src],
-            send_sem=g_send.at[dest],
-            recv_sem=g_recv.at[src],
+            src_ref=block_of(dest, side),
+            dst_ref=recv.at[src, side],
+            send_sem=g_send.at[2 * dest + side],
+            recv_sem=g_recv.at[2 * src + side],
             device_id=(dest, t),
             device_id_type=MESH,
         )
 
-    own_grad = pltpu.make_async_copy(block_of(d), recv.at[d], load_sem.at[11])
-
-    def send_block(dest):
+    def own_grad(side):
+        return pltpu.make_async_copy(block_of(d, side), recv.at[d, side], load_sem.at[11 + side])
+
+    def send_block(dest, side):
         @pl.when(dest != d)
         def _():
-            grad_copy(dest, d).start()
+            grad_copy(dest, d, side).start()
 
         @pl.when(dest == d)
         def _():
-            own_grad.start()
+            own_grad(side).start()
 
     def tiles_of(which, start, stop):
         lax.fori_loop(which * half_tiles + start, which * half_tiles + stop, tile, 0)
@@ -121,7 +123,8 @@
     for load in loads[:3]:
         load.wait()
     tiles_of(first, 0, head)
-    send_block(first * half)
+    for side in (0, 1):
+        send_block(first * half, side)
 
     for load in loads[3:6]:
         load.wait()
@@ -130,10 +133,12 @@
         need = -(-((j + 1) * rows) // 128)
         tiles_of(first, done, need)
         done = need
-        if j < 2:
-            send_block(first * half + j)
-        else:
-            pl.when(inner == 0)(functools.partial(send_block, first * half + j))
+        for side in (0, 1):
+            send = functools.partial(send_block, first * half + j, side)
+            if 2 * j + side < HELD:
+                send()
+            else:
+                pl.when(inner == 0)(send)
     for load in loads[6:]:
         load.wait()
     tiles_of(1 - first, 0, half_tiles)
@@ -182,10 +187,14 @@
         zz = (z + k) % nz
         piece_copy(d, t, xz_send.at[zz], (zz * 2 + c, t)).start()
 
-    for j in range(2, half):
-        pl.when(inner == 1)(functools.partial(send_block, first * half + j))
     for j in range(half):
-        send_block((1 - first) * half + j)
+        for side in (0, 1):
+            if 2 * j + side >= HELD:
+                send = functools.partial(send_block, first * half + j, side)
+                pl.when(inner == 1)(send)
+    for j in range(half):
+        for side in (0, 1):
+            send_block((1 - first) * half + j, side)
 
     if nz == 4:
         order = [z, z + 1 - 2 * (z % 2), 3 - 3 * (z // 2), 2 - z // 2]
@@ -221,14 +230,14 @@
 
     for k, zz in enumerate(order):
         core_copy(zz, 1 - c).wait_recv()
-        if k == 0:
-            own_grad.wait()
-            grad_copy(d, partner).wait_recv()
-        else:
-            grad_copy(d, zz * 2).wait_recv()
-            grad_copy(d, zz * 2 + 1).wait_recv()
         xp = xp_all[pl.ds(pl.multiple_of(zz * 2 * grp, 128), 2 * grp), :]
         for part_of in (0, 1):
+            if k == 0:
+                own_grad(part_of).wait()
+                grad_copy(d, partner, part_of).wait_recv()
+            else:
+                grad_copy(d, zz * 2, part_of).wait_recv()
+                grad_copy(d, zz * 2 + 1, part_of).wait_recv()
             lhs = jnp.concatenate([recv[zz * 2, part_of], recv[zz * 2 + 1, part_of]], axis=1)
             term = jnp.dot(lhs, xp, preferred_element_type=jnp.float32)
             at = slice(part_of * rank, (part_of + 1) * rank)
@@ -249,7 +258,8 @@
     for zz in range(nz):
         core_copy(zz, c).wait_send()
     for k in range(1, ndp):
-        grad_copy((d + k) % ndp, d).wait_send()
+        for side in (0, 1):
+            grad_copy((d + k) % ndp, d, side).wait_send()
 
 
 def exchange(ndp, nt, tokens_in, projector, gate_pre, up_pre, hidden_grad):
@@ -278,7 +288,7 @@
             pltpu.VMEM((grp * ndp, rank), bf),
             pltpu.VMEM((2, cols, grp), bf),
             pltpu.VMEM((ndp, 2, rows, grp), bf),
-            dma((12,)),
+            dma((13,)),
             dma((nt,)),
             dma((nt,)),
             dma((nt,)),
@@ -288,8 +298,8 @@
             dma((nz,)),
             dma((ndp * nt,)),
             dma((nz,)),
-            dma((ndp,)),
-            dma((ndp,)),
+            dma((2 * ndp,)),
+            dma((2 * ndp,)),
         ],
         compiler_params=pltpu.CompilerParams(
             collective_id=0, has_side_effects=True, vmem_limit_bytes=32 * 1024 * 1024
@@ -330,11 +340,43 @@
     return (m_next, v_next, direction)
 
 
+def finish_kernel(total_tokens, steps, sum_ref, m_ref, v_ref, *refs):
+    outs, bufs, sem = refs[:3], refs[3:6], refs[6]
+    rows = sum_ref.shape[0] // steps
+    copies = []
+    for i in range(steps):
+        at = slice(i * rows, (i + 1) * rows)
+        values = finish(sum_ref[at, :], total_tokens, m_ref[at, :], v_ref[at, :])
+        for k in range(3):
+            bufs[k][at, :] = values[k]
+            copy = pltpu.make_async_copy(
+                bufs[k].at[at, :], outs[k].at[at, :], sem.at[3 * i + k]
+            )
+            copy.start()
+            copies.append(copy)
+    for copy in copies:
+        copy.wait()
+
+
+def finish_call(summed, total_tokens, moment_m, moment_v):
+    steps = 6
+    shape = jax.ShapeDtypeStruct(summed.shape, jnp.float32)
+    return pl.pallas_call(
+        functools.partial(finish_kernel, total_tokens, steps),
+        out_shape=(shape,) * 3,
+        in_specs=[pl.BlockSpec(memory_space=pltpu.VMEM)] * 3,
+        out_specs=[pl.BlockSpec(memory_space=pltpu.HBM)] * 3,
+        scratch_shapes=[pltpu.VMEM(summed.shape, jnp.float32)] * 3
+        + [pltpu.SemaphoreType.DMA((3 * steps,))],
+        compiler_params=pltpu.CompilerParams(vmem_limit_bytes=16 * 1024 * 1024),
+    )(summed, moment_m, moment_v)
+
+
 def local(tokens_in, projector, gate_pre, up_pre, hidden_grad, moment_m, moment_v):
     ndp, nt = lax.axis_size("dp"), lax.axis_size("tensor")
     if fits(ndp, nt, tokens_in, projector, gate_pre):
         summed = exchange(ndp, nt, tokens_in, projector, gate_pre, up_pre, hidden_grad)
-        return finish(summed, gate_pre.shape[0] * ndp, moment_m, moment_v)
+        return tuple(finish_call(summed, gate_pre.shape[0] * ndp, moment_m, moment_v))
     gate = gate_pre.astype(jnp.float32)
     hgrad = hidden_grad.astype(jnp.float32)
     sig = jax.nn.sigmoid(gate)

time: 57.1 us -> 54.9 us (0.961)
  the two profiles are of different devices: /device:TPU:25 before, /device:TPU:0 now
where the time goes in v5:
time: 54.9 us; the launch traced here: 54.7 us
  Pallas kernels  54 us (98%)
  between operations  0.67 us (1%)
    pallas_call x1, Pallas kernels, exchange(): pl.pallas_call(functools.partial(exchange_kernel, ndp, nt), out_shape=jax...  51.2 us
    pallas_call x1, Pallas kernels, finish_call(): pl.pallas_call(functools.partial(finish_kernel, total_tokens, steps), out...  2.79 us

profile of v5, /device:TPU:0, one launch (start us, length us, event | category | flops | bytes accessed | tf_op | source)
XLA Modules:
  0.0 54.7 jit_solution(17368524137863462262)
XLA Ops:
  0.6 0.0 copy-start.1
  0.6 0.0 copy-start
  0.7 51.2 %shard_map.94.sum_ref = f32[480,1024]{1,0:T(8,128)S(1)} custom-call(bf16[32,8192]{1,0:T(8,128)(2,1)} %tok_ref.1, bf16[2048,512]{1,0:T(8,128)(2,1)} %prj_ref.1, bf16[128,3840]{1,0:T(8,128)(2,1)} %gate_ref.1, bf16[128,3840]{1,0:T(8,128)(2,1)} %up_ref.1, bf16[128,3840]{1,0:T(8,128)(2,1)} %hg_ref.1), custom_call_target="tpu_custom_call" | custom-call | flops 1275068416 | bytes 3932160 | tf_op jit(solution)/shard_map/pallas_call | solution.py:275
  51.9 0.0 copy-done.1
  51.9 0.0 copy-done
  51.9 2.8 %shard_map.95 = (f32[480,1024]{1,0:T(8,128)}, f32[480,1024]{1,0:T(8,128)}, f32[480,1024]{1,0:T(8,128)}) custom-call(f32[480,1024]{1,0:T(8,128)S(1)} %shard_map.94.sum_ref, f32[480,1024]{1,0:T(8,128)S(1)} %copy-done, f32[480,1024]{1,0:T(8,128)S(1)} %copy-done.1), custom_call_target="tpu_custom_call" | custom-call | tf_op jit(solution)/shard_map/pallas_call | solution.py:364
Async XLA Ops:
  0.6 51.2 %copy-start.1 = (f32[480,1024]{1,0:T(8,128)S(1)}, f32[480,1024]{1,0:T(8,128)}, u32[]{:S(2)}) copy-start(f32[480,1024]{1,0:T(8,128)} %v_ref.1) | copy-start | bytes 5898244
  0.6 51.2 %copy-start = (f32[480,1024]{1,0:T(8,128)S(1)}, f32[480,1024]{1,0:T(8,128)}, u32[]{:S(2)}) copy-start(f32[480,1024]{1,0:T(8,128)} %m_ref.1) | copy-start | bytes 5898244

commit v6 on v5

--- a/solution.py
+++ b/solution.py
@@ -117,12 +117,12 @@
     def tiles_of(which, start, stop):
         lax.fori_loop(which * half_tiles + start, which * half_tiles + stop, tile, 0)
 
-    pl.semaphore_wait(barrier, ndp + nt - 2)
-    for k in range(1, nt):
-        tok_copy((t + k) % nt, t).start()
     for load in loads[:3]:
         load.wait()
     tiles_of(first, 0, head)
+    pl.semaphore_wait(barrier, ndp + nt - 2)
+    for k in range(1, nt):
+        tok_copy((t + k) % nt, t).start()
     for side in (0, 1):
         send_block(first * half, side)
 

time: 54.9 us -> 54.6 us (level)
  no operation moved by 1% of the time
where the time goes in v6:
time: 54.6 us; the launch traced here: 54.3 us
  Pallas kernels  53.6 us (98%)
  between operations  0.67 us (1%)
    pallas_call x1, Pallas kernels, exchange(): pl.pallas_call(functools.partial(exchange_kernel, ndp, nt), out_shape=jax...  50.8 us
    pallas_call x1, Pallas kernels, finish_call(): pl.pallas_call(functools.partial(finish_kernel, total_tokens, steps), out...  2.79 us

profile of v6, /device:TPU:0, one launch (start us, length us, event | category | flops | bytes accessed | tf_op | source)
XLA Modules:
  0.0 54.3 jit_solution(10814501026351904075)
XLA Ops:
  0.6 0.0 copy-start.1
  0.6 0.0 copy-start
  0.7 50.8 %shard_map.94.sum_ref = f32[480,1024]{1,0:T(8,128)S(1)} custom-call(bf16[32,8192]{1,0:T(8,128)(2,1)} %tok_ref.1, bf16[2048,512]{1,0:T(8,128)(2,1)} %prj_ref.1, bf16[128,3840]{1,0:T(8,128)(2,1)} %gate_ref.1, bf16[128,3840]{1,0:T(8,128)(2,1)} %up_ref.1, bf16[128,3840]{1,0:T(8,128)(2,1)} %hg_ref.1), custom_call_target="tpu_custom_call" | custom-call | flops 1275068416 | bytes 3932160 | tf_op jit(solution)/shard_map/pallas_call | solution.py:275
  51.5 0.0 copy-done.1
  51.5 0.0 copy-done
  51.5 2.8 %shard_map.95 = (f32[480,1024]{1,0:T(8,128)}, f32[480,1024]{1,0:T(8,128)}, f32[480,1024]{1,0:T(8,128)}) custom-call(f32[480,1024]{1,0:T(8,128)S(1)} %shard_map.94.sum_ref, f32[480,1024]{1,0:T(8,128)S(1)} %copy-done, f32[480,1024]{1,0:T(8,128)S(1)} %copy-done.1), custom_call_target="tpu_custom_call" | custom-call | tf_op jit(solution)/shard_map/pallas_call | solution.py:364
Async XLA Ops:
  0.6 50.8 %copy-start.1 = (f32[480,1024]{1,0:T(8,128)S(1)}, f32[480,1024]{1,0:T(8,128)}, u32[]{:S(2)}) copy-start(f32[480,1024]{1,0:T(8,128)} %v_ref.1) | copy-start | bytes 5898244
  0.6 50.8 %copy-start = (f32[480,1024]{1,0:T(8,128)S(1)}, f32[480,1024]{1,0:T(8,128)}, u32[]{:S(2)}) copy-start(f32[480,1024]{1,0:T(8,128)} %m_ref.1) | copy-start | bytes 5898244
